TPU v7x, 128 devices: a whole 4x4x4 slice. The times are simulated.
128 devices in a mesh: grp: 4 (over y), atom: 32 (over x, z, core).
Axes of the slice: x: 4, y: 4, z: 4, core: 2. Of those that a mesh axis runs over, the one named last changes fastest.
Arguments:
- tokens: bfloat16 [512, 8192], P(('grp', 'atom')), may hold values from -6 to 6
- dictionary: bfloat16 [32, 2048, 8192], P('atom', None, 'grp'), may hold values from -0.03125 to 0.03125
- candidates: int32 [512, 8], P(('grp', 'atom')), may hold values from 0 to 31, all different within a row; in each aligned block of 4 rows (0 to 3, 4 to 7, ...) at most 2 rows name the same one
Outputs:
- residual: float32 [512, 8192], P(('grp', 'atom'))
- codes: float32 [32, 256, 2048], P('atom', None, 'grp')
Inputs may be any that keep to these rules, and one draw needn't show every extreme that they name: `candidates`: each token names 8 different blocks. Among the 4 tokens of one shard (tokens s * 4 to (s + 1) * 4 - 1) no block is named by more than 2 tokens, and some block is named by exactly 2. Every block is named by some token.
All inputs are finite; a program needn't handle non-finite values.
Results may differ from a plain program's by a relative error of at most 0.02.
Values may be sent and summed in bfloat16 or wider, within the bound.
A program may use at most 64 MiB of HBM per device.

v0:
```python
import jax
import jax.numpy as jnp
from jax import lax
from jax.sharding import PartitionSpec as P

ITERS = 2


step_size = 1.6
sparsity = 0.125


def per_device(tokens, dictionary, candidates):
    groups = lax.axis_size("grp")
    blocks = lax.axis_size("atom")
    devices = groups * blocks
    tok_rows, features = tokens.shape
    top_count = candidates.shape[1]
    atom_count = dictionary.shape[1]
    quarter = dictionary.shape[2]
    capacity = min(tok_rows, max(2, 2 * tok_rows * top_count // blocks))
    table_rows = devices * capacity
    share_width = atom_count // groups
    block_ids = jnp.arange(blocks, dtype=jnp.int32)
    member = jnp.sum((candidates[:, :, None] == block_ids).astype(jnp.int32), axis=1)
    before = jnp.cumsum(member, axis=0) - member
    slot_ids = jnp.arange(capacity, dtype=jnp.int32)
    chosen = (member.T[:, None, :] > 0) & (before.T[:, None, :] == slot_ids[None, :, None])
    select = chosen.astype(jnp.bfloat16)
    weights = dictionary[0]
    initial = tokens.astype(jnp.float32)
    residual = initial
    outbound = tokens
    code_whole = jnp.zeros((table_rows, atom_count), jnp.float32)
    for iteration in range(ITERS):
        feature_parts = outbound.reshape(tok_rows, groups, quarter)
        outgoing = jnp.einsum(
            "bct,tqd->qbcd", select, feature_parts, preferred_element_type=jnp.float32
        ).astype(jnp.bfloat16)
        arrived = lax.all_to_all(
            outgoing.reshape(devices, capacity, quarter),
            ("grp", "atom"),
            split_axis=0,
            concat_axis=0,
            tiled=True,
        )
        arrived_rows = arrived.reshape(table_rows, quarter)
        partial_value = lax.dot_general(
            arrived_rows, weights, (((1,), (1,)), ((), ())), preferred_element_type=jnp.float32
        )
        partial_bf = partial_value.astype(jnp.bfloat16)
        gradient = lax.psum(partial_bf, "grp").astype(jnp.float32)
        code_whole = jnp.maximum(code_whole + step_size * (gradient - sparsity), 0.0)
        code_bf = code_whole.astype(jnp.bfloat16)
        rebuilt_part = jnp.dot(code_bf, weights, preferred_element_type=jnp.float32).astype(
            jnp.bfloat16
        )
        returned = lax.all_to_all(
            rebuilt_part.reshape(devices, capacity, quarter),
            ("grp", "atom"),
            split_axis=0,
            concat_axis=0,
            tiled=True,
        )
        returned = returned.reshape(groups, blocks, capacity, quarter)
        rebuilt_sum = jnp.einsum(
            "bct,qbcd->tqd", select, returned, preferred_element_type=jnp.float32
        )
        residual = initial - rebuilt_sum.reshape(tok_rows, features)
        outbound = residual.astype(jnp.bfloat16)
    codes_out = lax.dynamic_slice_in_dim(
        code_whole, lax.axis_index("grp") * share_width, share_width, 1
    )
    return (residual, codes_out[None])


def solution(mesh):
    placed = (P(("grp", "atom"), None), P("atom", None, "grp"), P(("grp", "atom"), None))
    return jax.shard_map(
        per_device,
        mesh=mesh,
        in_specs=placed,
        out_specs=(P(("grp", "atom"), None), P("atom", None, "grp")),
        check_vma=False,
    )
```

profile of v0, /device:TPU:0, one launch (start us, length us, event | category | flops | bytes accessed | tf_op | source)
XLA Modules:
  0.0 247.4 jit_solution(13072677737393702819)
XLA Ops:
  7.2 0.0 all-reduce.3.cloned.1.call-start
  7.2 0.8 convert_reduce_fusion
  8.0 1.3 convolution_convert_fusion.1
  9.4 1.1 copy.30
  10.5 30.2 %all_to_all.20 = bf16[128,2,2048]{2,1,0:T(2,128)(2,1)S(1)} all-to-all(bf16[128,2,2048]{2,1,0:T(2,128)(2,1)S(1)} %copy.30), channel_id=1, replica_groups=mesh['grp'=4,'atom'=32] {'grp','atom'}, dimensions={0} | all-to-all | bytes 2097152 | tf_op jit(solution)/shard_map/all_to_all | solution.py:40
  40.7 0.4 reshape.44
  41.1 6.8 %fusion.11 = bf16[256,2048]{1,0:T(8,128)(2,1)} fusion(bf16[256,2048]{1,0:T(8,128)(2,1)S(1)} %reshape.44, bf16[1,2048,2048]{2,1,0:T(8,128)(2,1)} %param.4), kind=kOutput, calls=%fused_computation.13 | convolution fusion | flops 2148007936 | bytes 10485760 | tf_op jit(solution)/shard_map/dot_general | solution.py:48
  47.9 0.0 all-reduce.3.cloned.1.call-update
  48.0 0.0 all-reduce.5.cloned.1.call-start
  48.0 41.7 %all-reduce.3.cloned.1.call-done = bf16[256,2048]{1,0:T(8,128)(2,1)} async-done(((bf16[256,2048]{1,0:T(8,128)(2,1)}), bf16[256,2048]{1,0:T(8,128)(2,1)}) %all-reduce.3.cloned.1.call-update) | async-done | bytes 1048592 | tf_op jit(solution)/shard_map/psum | solution.py:52
  89.7 6.1 %fusion.14 = bf16[256,2048]{1,0:T(8,128)(2,1)S(1)} fusion(bf16[1,2048,2048]{2,1,0:T(8,128)(2,1)} %param.4, bf16[256,2048]{1,0:T(8,128)(2,1)} %all-reduce.3.cloned.1.call-done), kind=kOutput, calls=%fused_computation.14 | convolution fusion | flops 2150629376 | bytes 10485760 | tf_op jit(solution)/shard_map/dot_general | solution.py:55
  95.8 0.7 reshape.45
  96.5 28.7 %all_to_all.21 = bf16[128,2,2048]{2,1,0:T(2,128)(2,1)S(1)} all-to-all(bf16[128,2,2048]{2,1,0:T(2,128)(2,1)S(1)} %reshape.45), channel_id=1, replica_groups=mesh['grp'=4,'atom'=32] {'grp','atom'}, dimensions={0} | all-to-all | bytes 2097152 | tf_op jit(solution)/shard_map/all_to_all | solution.py:58
  125.2 0.0 copy-start.2
  125.2 0.8 copy.41
  126.0 0.8 dot_general.36
  126.8 0.0 copy-done.2
  126.8 0.3 fusion.2
  127.2 0.5 fusion.23
  127.7 0.1 copy.33
  127.7 1.1 copy.34
  128.8 23.4 %all_to_all.22 = bf16[128,2,2048]{2,1,0:T(2,128)(2,1)S(1)} all-to-all(bf16[128,2,2048]{2,1,0:T(2,128)(2,1)S(1)} %copy.34), channel_id=1, replica_groups=mesh['grp'=4,'atom'=32] {'grp','atom'}, dimensions={0} | all-to-all | bytes 2097152 | tf_op jit(solution)/shard_map/all_to_all | solution.py:40
  152.2 0.4 reshape.49
  152.6 0.0 copy-start
  152.6 6.8 %fusion.17 = bf16[256,2048]{1,0:T(8,128)(2,1)} fusion(bf16[256,2048]{1,0:T(8,128)(2,1)S(1)} %reshape.49, bf16[1,2048,2048]{2,1,0:T(8,128)(2,1)} %param.4), kind=kOutput, calls=%fused_computation.15 | convolution fusion | flops 2148007936 | bytes 10485760 | tf_op jit(solution)/shard_map/dot_general | solution.py:48
  159.4 0.0 all-reduce.5.cloned.1.call-update
  159.5 41.8 %all-reduce.5.cloned.1.call-done = bf16[256,2048]{1,0:T(8,128)(2,1)} async-done(((bf16[256,2048]{1,0:T(8,128)(2,1)}), bf16[256,2048]{1,0:T(8,128)(2,1)}) %all-reduce.5.cloned.1.call-update) | async-done | bytes 1048592 | tf_op jit(solution)/shard_map/psum | solution.py:52
  201.3 0.0 copy-done
  201.3 6.3 %fusion.20 = bf16[256,2048]{1,0:T(8,128)(2,1)S(1)} fusion(bf16[1,2048,2048]{2,1,0:T(8,128)(2,1)} %param.4, bf16[256,2048]{1,0:T(8,128)(2,1)} %all-reduce.5.cloned.1.call-done, bf16[256,2048]{1,0:T(8,128)(2,1)S(1)} %copy-done), kind=kOutput, calls=%fused_computation.16 | convolution fusion | flops 2153250816 | bytes 11534336 | tf_op jit(solution)/shard_map/dot_general | solution.py:55
  207.5 0.0 copy-start.1
  207.5 1.5 reshape.50
  209.1 9.6 %all-to-all-start.3 = ((bf16[128,2,2048]{2,1,0:T(2,128)(2,1)}), bf16[128,2,2048]{2,1,0:T(2,128)(2,1)S(1)}, u32[]{:S(2)}, u32[]{:S(2)}) async-start(bf16[128,2,2048]{2,1,0:T(2,128)(2,1)} %reshape.50), calls=%async_computation.3 | async-start | bytes 2097152 | tf_op jit(solution)/shard_map/all_to_all | solution.py:58
  218.7 0.0 copy-done.1
  218.7 0.6 add_maximum_fusion
  219.3 0.8 dynamic-slice_bitcast_fusion
  220.1 17.8 %all-to-all-done.3 = bf16[128,2,2048]{2,1,0:T(2,128)(2,1)S(1)} async-done(((bf16[128,2,2048]{2,1,0:T(2,128)(2,1)}), bf16[128,2,2048]{2,1,0:T(2,128)(2,1)S(1)}, u32[]{:S(2)}, u32[]{:S(2)}) %all-to-all-start.3) | async-done | bytes 1048608 | tf_op jit(solution)/shard_map/all_to_all | solution.py:58
  237.9 0.8 copy.40
  238.7 0.8 dot_general.42
  239.6 1.0 fusion
  (4 shorter events, 0.1 us)
Async XLA Ops:
  7.2 82.6 %all-reduce.3.cloned.1.call-start = ((), (), s32[]{:S(2)}) async-start(), calls=%async_computation.4 | async-start | bytes 2097152 | tf_op jit(solution)/shard_map/psum | solution.py:52
  48.0 153.3 %all-reduce.5.cloned.1.call-start = ((), (), s32[]{:S(2)}) async-start(), calls=%async_computation.5 | async-start | bytes 2097152 | tf_op jit(solution)/shard_map/psum | solution.py:52
  125.2 1.6 copy-start.2
  152.6 48.6 %copy-start = (bf16[256,2048]{1,0:T(8,128)(2,1)S(1)}, bf16[256,2048]{1,0:T(8,128)(2,1)}, u32[]{:S(2)}) copy-start(bf16[256,2048]{1,0:T(8,128)(2,1)} %all-reduce.3.cloned.1.call-done) | copy-start | bytes 3145732
  207.5 11.1 %copy-start.1 = (bf16[256,2048]{1,0:T(8,128)(2,1)S(1)}, bf16[256,2048]{1,0:T(8,128)(2,1)}, u32[]{:S(2)}) copy-start(bf16[256,2048]{1,0:T(8,128)(2,1)} %all-reduce.5.cloned.1.call-done) | copy-start | bytes 3145732
  209.1 28.9 %all-to-all-start.3 = ((bf16[128,2,2048]{2,1,0:T(2,128)(2,1)}), bf16[128,2,2048]{2,1,0:T(2,128)(2,1)S(1)}, u32[]{:S(2)}, u32[]{:S(2)}) async-start(bf16[128,2,2048]{2,1,0:T(2,128)(2,1)} %reshape.50), calls=%async_computation.3 | async-start | bytes 2097152 | tf_op jit(solution)/shard_map/all_to_all | solution.py:58
Sparse Core Ops, SparseCore 0:
  48.1 41.6 all-reduce.2
  159.6 41.6 all-reduce.4
where the time goes:
time: 248 us; the launch traced here: 247 us
  waiting for transfers between devices  101 us (41%)
  blocking collectives  82.3 us (33%)
  matrix products  29.1 us (12%)
  between operations  14.2 us (6%)
  starting transfers between devices  9.67 us (4%)
  local copies, waits for them, and re-layouts  9.41 us (4%)
    psum x2, waiting for transfers between devices, per_device(): gradient = lax.psum(partial_bf, 'grp').astype(jnp.float32)  83.5 us
    all_to_all x2, blocking collectives, per_device(): lax.all_to_all(outgoing.reshape(devices, capacity, quarter), ('grp', 'ato...  53.6 us
    all_to_all x1, blocking collectives, per_device(): lax.all_to_all(rebuilt_part.reshape(devices, capacity, quarter), ('grp',...  28.7 us
    all_to_all x1, waiting for transfers between devices, per_device(): lax.all_to_all(rebuilt_part.reshape(devices, capacity, quarter), ('grp',...  17.8 us
    dot_general x2, matrix products, per_device(): lax.dot_general(arrived_rows, weights, (((1,), (1,)), ((), ())), preferre...  13.6 us
    dot_general x2, matrix products, per_device(): jnp.dot(code_bf, weights, preferred_element_type=jnp.float32)  12.3 us
    all_to_all x1, starting transfers between devices, per_device(): lax.all_to_all(rebuilt_part.reshape(devices, capacity, quarter), ('grp',...  9.59 us
  transfers between devices with their start and end apart: 3, of which 3 were waited for; matrix products, arithmetic and copies ran while one was open for 1% of the time, Pallas kernels for 0%

commit v1 on v0

v1 whole, which is shorter than its diff:
```python
import jax
import jax.numpy as jnp
from jax import lax
from jax.experimental import pallas as pl
from jax.experimental.pallas import tpu as pltpu
from jax.sharding import PartitionSpec as P

ITERS = 2
CHAINS = 1
STEP = 1.6
SPARSITY = 0.125
MESH = pl.DeviceIdType.MESH
SHIFT = (0, 3, 1, 2)
BF = jnp.bfloat16
F32 = jnp.float32
N_SEMS = 260
LANES = 128


def nt_dot(a, b):
    return lax.dot_general(a, b, (((1,), (1,)), ((), ())), preferred_element_type=F32)


def nn_dot(a, b):
    return jnp.dot(a, b, preferred_element_type=F32)


def source(me, position):
    shift = jnp.where(position == 1, 3, jnp.where(position == 2, 1, jnp.where(position == 3, 2, 0)))
    return (me + shift) % 4


class Net:
    def __init__(self, send, recv):
        self.send, self.recv, self.count, self.open = send, recv, 0, []

    def copy(self, src, dst, device):
        n = self.count
        self.count += 1
        made = pltpu.make_async_remote_copy(
            src_ref=src,
            dst_ref=dst,
            send_sem=self.send.at[n],
            recv_sem=self.recv.at[n],
            device_id=device,
            device_id_type=MESH,
        )
        made.start()
        self.open.append(made)
        return made

    def finish(self):
        for made in self.open:
            made.wait_send()


def body(names, *refs):
    r = dict(zip(names, refs))
    tok, dict_hbm, res_out, codes = r["tok"], r["dict"], r["res"], r["codes"]
    weights = r["weights"]
    y, atom = lax.axis_index("grp"), lax.axis_index("atom")
    x, z, core = atom // 8, (atom // 2) % 4, atom % 2
    tokens_in = 16 // CHAINS
    shards_in = 4 // CHAINS
    rows = 256 // CHAINS
    gathered = 32 * tokens_in
    half = gathered // 2

    load = pltpu.make_async_copy(dict_hbm.at[0], weights, r["wsem"])
    load.start()

    def device(nx, nz, nc):
        return {"atom": nx * 8 + nz * 2 + nc}

    minus = {"x": device((x + 3) % 4, z, core), "z": device(x, (z + 3) % 4, core), "y": {"grp": (y + 3) % 4}}
    plus = {"x": device((x + 1) % 4, z, core), "z": device(x, (z + 1) % 4, core), "y": {"grp": (y + 1) % 4}}
    partner = device(x, z, 1 - core)
    opposite = {"grp": (y + 2) % 4}

    barrier = pltpu.get_barrier_semaphore()
    others = [minus["x"], plus["x"], minus["z"], plus["z"], minus["y"], plus["y"], opposite, partner]
    for other in others:
        pl.semaphore_signal(barrier, inc=1, device_id=other, device_id_type=MESH)
    pl.semaphore_wait(barrier, len(others))

    net = Net(r["send"], r["recv"])

    first = r["first"]
    swaps = []
    for position in (1, 2, 3):
        target = (y + SHIFT[position]) % 4
        swaps.append(net.copy(tok.at[target], first.at[y], {"grp": target}))
    first[y] = tok[y]

    lo, hi = pl.ds(0, 256), pl.ds(256, 256)

    def gather(big):
        st = []
        for h in range(2):
            g = big[h]
            width = g.shape[-1]
            cut = (width // 2 + LANES - 1) // LANES * LANES
            left, right = pl.ds(0, cut), pl.ds(cut, width - cut)
            full = pl.ds(0, width)
            a, b = ("x", "z") if h == 0 else ("z", "x")

            def view(pa, pb, cols=full, owner=0, g=g, h=h):
                return g.at[owner, pa, pb, :, cols] if h == 0 else g.at[owner, pb, pa, :, cols]

            def share(pa, pb, view=view):
                return net.copy(view(pa, pb), view(pa, pb, owner=1), partner)

            st.append(dict(view=view, share=share, left=left, right=right, a=a, b=b, part=[]))
        mid, every = pl.ds(1, 2), pl.ds(0, 4)
        for s in st:
            v, a, b = s["view"], s["a"], s["b"]
            s["a1"] = net.copy(v(0, 0), v(1, 0), plus[a])
            s["a2"] = net.copy(v(0, 0), v(2, 0), minus[a])
            s["b1"] = net.copy(v(0, 0), v(0, 1), plus[b])
            s["b2"] = net.copy(v(0, 0), v(0, 2), minus[b])
            s["part"].append(s["share"](0, 0))
        yield
        for s in st:
            v, a, b, lf, rt = s["view"], s["a"], s["b"], s["left"], s["right"]
            s["a1"].wait_recv()
            s["fa1"] = net.copy(v(1, 0, lf), v(3, 0, lf), plus[a])
            s["a2"].wait_recv()
            s["fa2"] = net.copy(v(2, 0, rt), v(3, 0, rt), minus[a])
            s["n1"] = net.copy(v(mid, 0), v(mid, 1), plus[b])
            s["n2"] = net.copy(v(mid, 0), v(mid, 2), minus[b])
            s["part"].append(s["share"](mid, 0))
        for s in st:
            v, a, b, lf, rt = s["view"], s["a"], s["b"], s["left"], s["right"]
            s["b1"].wait_recv()
            s["fo1"] = net.copy(v(0, 1, lf), v(0, 3, lf), plus[b])
            s["b2"].wait_recv()
            s["fo2"] = net.copy(v(0, 2, rt), v(0, 3, rt), minus[b])
            s["part"].append(s["share"](0, mid))
        yield
        for s in st:
            v, a, b = s["view"], s["a"], s["b"]
            s["fa1"].wait_recv()
            s["fa2"].wait_recv()
            s["o1"] = net.copy(v(3, 0), v(3, 1), plus[b])
            s["o2"] = net.copy(v(3, 0), v(3, 2), minus[b])
            s["part"].append(s["share"](3, 0))
        yield
        for s in st:
            v, a, b, lf, rt = s["view"], s["a"], s["b"], s["left"], s["right"]
            s["n1"].wait_recv()
            s["fn1"] = net.copy(v(mid, 1, lf), v(mid, 3, lf), plus[b])
            s["n2"].wait_recv()
            s["fn2"] = net.copy(v(mid, 2, rt), v(mid, 3, rt), minus[b])
            s["part"].append(s["share"](mid, mid))
        yield
        for s in st:
            v, a, b, lf, rt = s["view"], s["a"], s["b"], s["left"], s["right"]
            s["o1"].wait_recv()
            s["fp1"] = net.copy(v(3, 1, lf), v(3, 3, lf), plus[b])
            s["o2"].wait_recv()
            s["fp2"] = net.copy(v(3, 2, rt), v(3, 3, rt), minus[b])
            s["part"].append(s["share"](3, mid))
        yield
        for s in st:
            for key in ("fo1", "fo2", "fn1", "fn2", "fp1", "fp2"):
                s[key].wait_recv()
            s["part"].append(s["share"](every, 3))
        yield
        for s in st:
            for made in s["part"]:
                made.wait_recv()

    def ring_sum(axis, view, opp, nbr, cols):
        cut = cols // 2
        left, right = pl.ds(0, cut), pl.ds(cut, cut)
        c_om = net.copy(view(3, left), opp.at[0], plus[axis])
        c_op = net.copy(view(3, right), opp.at[1], minus[axis])
        c_ph = net.copy(view(2, right), view_of(nbr, 0, right), plus[axis])
        c_ml = net.copy(view(1, left), view_of(nbr, 1, left), minus[axis])
        yield
        c_om.wait_recv()
        mine = view(2, left)
        mine[...] = (mine[...].astype(F32) + opp[0].astype(F32)).astype(BF)
        c_pl = net.copy(mine, view_of(nbr, 0, left), plus[axis])
        c_op.wait_recv()
        mine = view(1, right)
        mine[...] = (mine[...].astype(F32) + opp[1].astype(F32)).astype(BF)
        c_mh = net.copy(mine, view_of(nbr, 1, right), minus[axis])
        yield
        for made in (c_ph, c_ml, c_pl, c_mh):
            made.wait_recv()

    def view_of(nbr, side, cols):
        lead = (slice(None),) * (len(nbr.shape) - 2)
        return nbr.at[(side,) + lead + (cols,)]

    def make_selectors(k, sel, sel_t, big):
        tags = big[0][:, :, :, :, 1024:1152].reshape(gathered, LANES)

        def shard_of(g):
            px, pz = (g // (4 * tokens_in)) % 4, (g // tokens_in) % 4
            own = g // (16 * tokens_in)
            column = source(x, px) * 8 + source(z, pz) * 2 + (core + own) % 2
            return ((g // 4) % shards_in + k * shards_in) * 32 + column

        pick = (lax.broadcasted_iota(jnp.int32, (rows, LANES), 1) == atom).astype(BF)
        slot = nt_dot(pick, tags)
        p = lax.broadcasted_iota(jnp.int32, (rows, gathered), 0)
        g = lax.broadcasted_iota(jnp.int32, (rows, gathered), 1)
        hit = (shard_of(g) == p // 2 + k * (rows // 2)) & (slot == (p % 2).astype(F32))
        sel[...] = jnp.where(hit, 1.0, 0.0).astype(BF)
        q = lax.broadcasted_iota(jnp.int32, (half, rows), 1)
        g = lax.broadcasted_iota(jnp.int32, (half, rows), 0)
        same = shard_of(g) == q // 2 + k * (rows // 2)
        for side in range(2):
            block = atom if side == 0 else atom + 1 - 2 * core
            pick = (lax.broadcasted_iota(jnp.int32, (LANES, rows), 0) == block).astype(BF)
            slot = nn_dot(tags[:half], pick)
            hit = same & (slot == (q % 2).astype(F32))
            sel_t[:, side * rows : (side + 1) * rows] = jnp.where(hit, 1.0, 0.0).astype(BF)

    def chain(k):
        state = codes.at[pl.ds(k * rows, rows), :]
        sel, sel_t, start = r["sel"].at[k], r["sel_t"].at[k], r["start"].at[k]
        table, total = r["table"].at[k], r["total"].at[k]
        for it in range(ITERS):
            big = [r["g0a" if it == 0 else "g0b"].at[k], r["g1"].at[it, k]]
            part, opp, nbr = r["part"].at[it, k], r["y_opp"].at[it, k], r["y_nbr"].at[it, k]
            full, back, terms = r["full"].at[it, k], r["back"].at[it, k], r["terms"].at[it, k]
            if it == 0:
                pieces = [first[k * shards_in + j].astype(F32) for j in range(shards_in)]
                unit = jnp.concatenate(pieces, axis=0)
                start[:, :1024] = unit[:, :1024]
                start[:, 1024:] = unit[:, 1152:]
                unit = unit.astype(BF)
                big[0][0, 0, 0] = unit[:, :1152]
                big[1][0, 0, 0] = unit[:, 1152:]
            yield from gather(big)
            if it == 0:
                make_selectors(k, sel, sel_t, big)
            chosen = sel[...]
            for h in range(2):
                @pl.loop(0, 4)
                def _(n, h=h):
                    cols = pl.ds(pl.multiple_of(n * 256, 256), 256)
                    values = big[h][:, :, :, :, cols].reshape(gathered, 256)
                    out = pl.ds(pl.multiple_of(h * 1024 + n * 256, 256), 256)
                    table[:, out] = nn_dot(chosen, values).astype(BF)
            if it == 0 and k == 0:
                load.wait()

            def products(position):
                base = ((y + SHIFT[position]) % 4) * 512

                @pl.loop(0, 2)
                def _(n):
                    taken = weights[pl.ds(pl.multiple_of(base + n * 256, 256), 256), :]
                    cols = pl.ds(pl.multiple_of(n * 256, 256), 256)
                    part[position, :, cols] = nt_dot(table[...], taken).astype(BF)

            products(3)
            c_om = net.copy(part.at[3, :, lo], opp.at[0], plus["y"])
            c_op = net.copy(part.at[3, :, hi], opp.at[1], minus["y"])
            products(2)
            c_ph = net.copy(part.at[2, :, hi], nbr.at[0, :, hi], plus["y"])
            products(1)
            c_ml = net.copy(part.at[1, :, lo], nbr.at[1, :, lo], minus["y"])
            yield
            c_om.wait_recv()
            part[2, :, lo] = (part[2, :, lo].astype(F32) + opp[0].astype(F32)).astype(BF)
            c_pl = net.copy(part.at[2, :, lo], nbr.at[0, :, lo], plus["y"])
            c_op.wait_recv()
            part[1, :, hi] = (part[1, :, hi].astype(F32) + opp[1].astype(F32)).astype(BF)
            c_mh = net.copy(part.at[1, :, hi], nbr.at[1, :, hi], minus["y"])
            products(0)
            yield

            def update(cols):
                gradient = part[0, :, cols].astype(F32) + nbr[0, :, cols].astype(F32)
                gradient = gradient + nbr[1, :, cols].astype(F32)
                moved = STEP * (gradient - SPARSITY)
                if it > 0:
                    moved = moved + state[:, cols]
                moved = jnp.maximum(moved, 0.0)
                state[:, cols] = moved
                full[0, :, cols] = moved.astype(BF)

            c_ml.wait_recv()
            c_pl.wait_recv()
            update(lo)
            s1 = net.copy(full.at[0, :, lo], full.at[1, :, lo], plus["y"])
            c_ph.wait_recv()
            c_mh.wait_recv()
            update(hi)
            s2 = net.copy(full.at[0, :, hi], full.at[2, :, hi], minus["y"])
            s3 = net.copy(full.at[0, :, hi], full.at[1, :, hi], plus["y"])
            s4 = net.copy(full.at[0, :, lo], full.at[2, :, lo], minus["y"])

            def taken(position, cols):
                base = ((y + SHIFT[position]) % 4) * 512
                return weights[pl.ds(pl.multiple_of(base, 512), 512), cols]

            @pl.loop(0, 8)
            def _(n):
                cols = pl.ds(pl.multiple_of(n * 256, 256), 256)
                total[:, cols] = nn_dot(full[0], taken(0, cols))

            yield
            s1.wait_recv()
            f1 = net.copy(full.at[1, :, lo], full.at[3, :, lo], plus["y"])
            s2.wait_recv()
            f2 = net.copy(full.at[2, :, hi], full.at[3, :, hi], minus["y"])
            yield
            s3.wait_recv()
            s4.wait_recv()

            @pl.loop(0, 8)
            def _(n):
                cols = pl.ds(pl.multiple_of(n * 256, 256), 256)
                total[:, cols] += nn_dot(full[1], taken(1, cols)) + nn_dot(full[2], taken(2, cols))

            yield
            f1.wait_recv()
            f2.wait_recv()
            shared = []
            for quarter in range(4):
                @pl.loop(0, 2)
                def _(n, quarter=quarter):
                    cols = pl.ds(pl.multiple_of(quarter * 512 + n * 256, 256), 256)
                    done = total[:, cols] + nn_dot(full[3], taken(3, cols))
                    back[0, :, cols] = done.astype(BF)

                cols = pl.ds(quarter * 512, 512)
                shared.append(net.copy(back.at[0, :, cols], back.at[1, :, cols], partner))
            yield
            spread = sel_t[...]
            opp_t, nbr_t = r["t_opp"].at[it, k], r["t_nbr"].at[it, k]
            opp_u, nbr_u = r["u_opp"].at[it, k], r["u_nbr"].at[it, k]
            lines = r["lines"].at[it, k]
            sums = []
            for h in range(2):
                for made in shared[2 * h : 2 * h + 2]:
                    made.wait_recv()

                @pl.loop(0, 4)
                def _(n, h=h):
                    cols = pl.ds(pl.multiple_of(h * 1024 + n * 256, 256), 256)
                    both = nn_dot(spread[:, :rows], back[0, :, cols])
                    both = both + nn_dot(spread[:, rows:], back[1, :, cols])
                    out = pl.ds(pl.multiple_of(n * 256, 256), 256)
                    terms[h, :, :, :, out] = both.astype(BF).reshape(4, 4, tokens_in, 256)

                def term(position, cols, h=h):
                    if h == 0:
                        return terms.at[h, :, position, :, cols]
                    return terms.at[h, position, :, :, cols]

                step = ring_sum("z" if h == 0 else "x", term, opp_t.at[h], nbr_t.at[h], 1024)
                next(step)
                sums.append(step)
            yield
            for step in sums:
                next(step)
            yield
            small = []
            for h in range(2):
                for _ in sums[h]:
                    pass
                own = terms[h, :, 0] if h == 0 else terms[h, 0]
                line = own.astype(F32) + nbr_t[h, 0].astype(F32) + nbr_t[h, 1].astype(F32)
                lines[h] = line.astype(BF)

                def unit_of(position, cols, h=h):
                    return lines.at[h, position, :, cols]

                step = ring_sum("x" if h == 0 else "z", unit_of, opp_u.at[h], nbr_u.at[h], 1024)
                next(step)
                small.append(step)
            yield
            for step in small:
                next(step)
            yield
            for h in range(2):
                for _ in small[h]:
                    pass
                summed = lines[h, 0].astype(F32) + nbr_u[h, 0].astype(F32) + nbr_u[h, 1].astype(F32)
                residual = start[:, h * 1024 : (h + 1) * 1024] - summed
                if it + 1 < ITERS:
                    nxt = r["g0b"].at[k] if h == 0 else r["g1"].at[it + 1, k]
                    nxt[0, 0, 0] = residual.astype(BF)
                else:
                    for j in range(shards_in):
                        r["final"][k * shards_in + j, :, h * 1024 : (h + 1) * 1024] = residual[4 * j : 4 * j + 4]

    for made in swaps:
        made.wait_recv()
    runs = [chain(k) for k in range(CHAINS)]
    for run in runs:
        for _ in run:
            pass
    final, landed = r["final"], r["landed"]
    ends = []
    for position in (1, 2, 3):
        target = (y + SHIFT[position]) % 4
        ends.append(net.copy(final.at[target], landed.at[y], {"grp": target}))
    landed[y] = final[y]
    for made in ends:
        made.wait_recv()
    res_out[...] = landed[...]
    net.finish()


def scratch():
    t, rows, gathered = 16 // CHAINS, 256 // CHAINS, 512 // CHAINS
    c, i = CHAINS, ITERS
    v = pltpu.VMEM
    return dict(
        weights=v((2048, 2048), BF),
        first=v((4, 4, 2176), BF),
        start=v((c, t, 2048), F32),
        g0a=v((c, 2, 4, 4, t, 1152), BF),
        g0b=v((c, 2, 4, 4, t, 1024), BF),
        g1=v((i, c, 2, 4, 4, t, 1024), BF),
        sel=v((c, rows, gathered), BF),
        sel_t=v((c, gathered // 2, 2 * rows), BF),
        table=v((c, rows, 2048), BF),
        part=v((i, c, 4, rows, 512), BF),
        y_opp=v((i, c, 2, rows, 256), BF),
        y_nbr=v((i, c, 2, rows, 512), BF),
        full=v((i, c, 4, rows, 512), BF),
        total=v((c, rows, 2048), F32),
        back=v((i, c, 2, rows, 2048), BF),
        terms=v((i, c, 2, 4, 4, t, 1024), BF),
        t_opp=v((i, c, 2, 2, 4, t, 512), BF),
        t_nbr=v((i, c, 2, 2, 4, t, 1024), BF),
        lines=v((i, c, 2, 4, t, 1024), BF),
        u_opp=v((i, c, 2, 2, t, 512), BF),
        u_nbr=v((i, c, 2, 2, t, 1024), BF),
        final=v((4, 4, 2048), F32),
        landed=v((4, 4, 2048), F32),
        send=pltpu.SemaphoreType.DMA((N_SEMS,)),
        recv=pltpu.SemaphoreType.DMA((N_SEMS,)),
        wsem=pltpu.SemaphoreType.DMA,
    )


def per_device(tokens, dictionary, candidates):
    block_ids = jnp.arange(LANES, dtype=jnp.int32)
    member = jnp.any(candidates[:, :, None] == block_ids, axis=1).astype(jnp.int32)
    earlier = (jnp.arange(4)[:, None] > jnp.arange(4)[None, :]).astype(jnp.int32)
    before = jnp.sum(earlier[:, :, None] * member[None], axis=1)
    tags = jnp.where(member > 0, before, -1).astype(BF)
    parts = tokens.reshape(4, 4, 2048).swapaxes(0, 1)
    tok = jnp.concatenate(
        [parts[:, :, :1024], jnp.broadcast_to(tags, (4, 4, LANES)), parts[:, :, 1024:]], axis=2
    )
    shapes = scratch()
    names = ["tok", "dict", "res", "codes"] + list(shapes)
    vmem = pl.BlockSpec(memory_space=pltpu.VMEM)
    res, codes = pl.pallas_call(
        lambda *refs: body(names, *refs),
        out_shape=(
            jax.ShapeDtypeStruct((4, 4, 2048), F32),
            jax.ShapeDtypeStruct((256, 512), F32),
        ),
        in_specs=[vmem, pl.BlockSpec(memory_space=pl.ANY)],
        out_specs=(vmem, vmem),
        scratch_shapes=list(shapes.values()),
        compiler_params=pltpu.CompilerParams(
            collective_id=0, has_side_effects=True, vmem_limit_bytes=60 * 1024 * 1024
        ),
        name="sparse_code",
    )(tok, dictionary)
    return res.swapaxes(0, 1).reshape(4, 8192), codes[None]


def solution(mesh):
    placed = (P(("grp", "atom"), None), P("atom", None, "grp"), P(("grp", "atom"), None))
    return jax.shard_map(
        per_device,
        mesh=mesh,
        in_specs=placed,
        out_specs=(P(("grp", "atom"), None), P("atom", None, "grp")),
        check_vma=False,
    )
```

time: 248 us -> 145 us (0.58)
  Pallas kernels: 0 us -> 138 us
  waiting for transfers between devices: 101 us -> 0 us
  blocking collectives: 82.3 us -> 0 us
  matrix products: 29.1 us -> 0 us
  between operations: 14.2 us -> 0.65 us
  starting transfers between devices: 9.67 us -> 0 us
  local copies, waits for them, and re-layouts: 9.41 us -> 4.24 us
    pallas_call x0 -> x1, Pallas kernels: none -> 138 us  [per_device(): pl.pallas_call(lambda *refs: body(names, *refs), out_shape=(jax.ShapeDtyp...]
    psum x2 -> x0, waiting for transfers between devices: 83.5 us -> none  [per_device(): gradient = lax.psum(partial_bf, 'grp').astype(jnp.float32)]
    all_to_all x3 -> x0, blocking collectives: 82.3 us -> none  [the longest x2 53.6 us: per_device(): lax.all_to_all(outgoing.reshape(devices, capacity, quarter), ('grp', 'ato...]
    dot_general x8 -> x0, matrix products: 29.1 us -> none  [the longest x2 13.6 us: per_device(): lax.dot_general(arrived_rows, weights, (((1,), (1,)), ((), ())), preferre...]
    all_to_all x1 -> x0, waiting for transfers between devices: 17.8 us -> none  [per_device(): lax.all_to_all(rebuilt_part.reshape(devices, capacity, quarter), ('grp',...]
    all_to_all x1 -> x0, starting transfers between devices: 9.59 us -> none  [per_device(): lax.all_to_all(rebuilt_part.reshape(devices, capacity, quarter), ('grp',...]
    reshape x8 -> x0, local copies, waits for them, and re-layouts: 6.86 us -> none  [the longest x2 2.23 us: per_device(): rebuilt_part.reshape(devices, capacity, quarter)]
    unnamed x6 -> x2, local copies, waits for them, and re-layouts: 0.01 us -> 3.44 us
  transfers between devices with their start and end apart: 3 -> 0, of which waited for: 3 -> 0; matrix products, arithmetic and copies ran while one was open for 1% -> 0% of each run, Pallas kernels for 0% -> 0%
where the time goes in v1:
time: 145 us
  Pallas kernels  138 us (95%)
  local copies, waits for them, and re-layouts  4.24 us (3%)
  other arithmetic  1.54 us (1%)
    pallas_call x1, Pallas kernels, per_device(): pl.pallas_call(lambda *refs: body(names, *refs), out_shape=(jax.ShapeDtyp...  138 us
    unnamed x2, local copies, waits for them, and re-layouts  3.44 us

profile of v1, /device:TPU:0, one launch (start us, length us, event | category | flops | bytes accessed | tf_op | source)
XLA Modules:
  0.0 144.8 jit_solution(9979470006642023116)
XLA Ops:
  0.6 0.8 fusion
  1.4 0.1 multiply_reduce_fusion
  1.5 0.8 fusion.2
  2.3 0.7 pad_maximum_fusion.refs_0_
  3.0 138.4 %sparse_code.1 = (f32[4,4,2048]{2,1,0:T(4,128)}, f32[256,512]{1,0:T(8,128)}) custom-call(bf16[4,4,2176]{2,1,0:T(4,128)(2,1)} %pad_maximum_fusion.refs_0_, bf16[1,2048,2048]{2,1,0:T(8,128)(2,1)} %refs_1_.1), custom_call_target="tpu_custom_call" | custom-call | tf_op jit(solution)/shard_map/sparse_code/pallas_call | solution.py:460
  141.4 1.6 %copy.7 = f32[4,8192]{1,0:T(4,128)} copy(f32[4,8192]{1,0:T(4,128)} %bitcast.8) | data formatting | bytes 262144
  142.9 1.9 %copy.8 = f32[1,256,512]{2,1,0:T(8,128)} copy(f32[1,256,512]{2,1,0:T(8,128)} %bitcast.7) | data formatting | bytes 1048576
  (4 shorter events, 0.0 us)

commit v2 on v1

v2 whole, which is shorter than its diff:
```python
import jax
import jax.numpy as jnp
from jax import lax
from jax.experimental import pallas as pl
from jax.experimental.pallas import tpu as pltpu
from jax.sharding import PartitionSpec as P

ITERS = 2
CHAINS = 1
STEP = 1.6
SPARSITY = 0.125
MESH = pl.DeviceIdType.MESH
SHIFT = (0, 3, 1, 2)
BACK = (0, 2, 1, 3)
BF = jnp.bfloat16
F32 = jnp.float32
N_SEMS = 260
LANES = 128


def nt_dot(a, b):
    return lax.dot_general(a, b, (((1,), (1,)), ((), ())), preferred_element_type=F32)


def nn_dot(a, b):
    return jnp.dot(a, b, preferred_element_type=F32)


def source(me, position):
    shift = jnp.where(position == 1, 3, jnp.where(position == 2, 1, jnp.where(position == 3, 2, 0)))
    return (me + shift) % 4


class Net:
    def __init__(self, send, recv):
        self.send, self.recv, self.count, self.open = send, recv, 0, []

    def copy(self, src, dst, device):
        n = self.count
        self.count += 1
        made = pltpu.make_async_remote_copy(
            src_ref=src,
            dst_ref=dst,
            send_sem=self.send.at[n],
            recv_sem=self.recv.at[n],
            device_id=device,
            device_id_type=MESH,
        )
        made.start()
        self.open.append(made)
        return made

    def finish(self):
        for made in self.open:
            made.wait_send()


def body(names, *refs):
    r = dict(zip(names, refs))
    tok, dict_hbm, res_out, codes = r["tok"], r["dict"], r["res"], r["codes"]
    tags = r["tags"]
    weights = r["weights"]
    y, atom = lax.axis_index("grp"), lax.axis_index("atom")
    x, z, core = atom // 8, (atom // 2) % 4, atom % 2
    tokens_in = 16 // CHAINS
    shards_in = 4 // CHAINS
    rows = 256 // CHAINS
    gathered = 32 * tokens_in
    half = gathered // 2

    load = pltpu.make_async_copy(dict_hbm.at[0], weights, r["wsem"])
    load.start()

    def device(nx, nz, nc):
        return {"atom": nx * 8 + nz * 2 + nc}

    ring = {
        "x": [device((x + d) % 4, z, core) for d in SHIFT],
        "z": [device(x, (z + d) % 4, core) for d in SHIFT],
        "y": [{"grp": (y + d) % 4} for d in SHIFT],
    }
    minus = {axis: ring[axis][1] for axis in ring}
    plus = {axis: ring[axis][2] for axis in ring}
    partner = device(x, z, 1 - core)

    barrier = pltpu.get_barrier_semaphore()
    others = ring["x"][1:] + ring["z"][1:] + ring["y"][1:] + [partner]
    for other in others:
        pl.semaphore_signal(barrier, inc=1, device_id=other, device_id_type=MESH)

    lane = lax.broadcasted_iota(jnp.int32, (4, LANES), 1)
    row = lax.broadcasted_iota(jnp.int32, (4, LANES), 0)
    named = jnp.zeros((4, LANES), jnp.int32)
    for k in range(8):
        named = named + jnp.where(r["cand"][:, k : k + 1] == lane, 1, 0)
    before = jnp.zeros((4, LANES), jnp.int32)
    for t in range(3):
        before = before + jnp.where(row > t, named[t : t + 1], 0)
    tags[...] = jnp.where(named > 0, before, -1).astype(F32).astype(BF)
    pl.semaphore_wait(barrier, len(others))

    net = Net(r["send"], r["recv"])

    first = r["first"]
    swaps = []
    for position in (1, 2, 3):
        target = (y + SHIFT[position]) % 4
        cols = pl.ds(pl.multiple_of(target * 2048, 2048), 2048)
        swaps.append(net.copy(tok.at[:, cols], first.at[y, :, pl.ds(0, 2048)], ring["y"][position]))
        swaps.append(net.copy(tags, first.at[y, :, pl.ds(2048, LANES)], ring["y"][position]))
    first[y, :, :2048] = tok[:, pl.ds(pl.multiple_of(y * 2048, 2048), 2048)]
    first[y, :, 2048:] = tags[...]

    lo, hi = pl.ds(0, 256), pl.ds(256, 256)

    def gather(big):
        st = []
        for h in range(2):
            g = big[h]
            a, b = ("x", "z") if h == 0 else ("z", "x")

            def view(pa, pb, owner=0, g=g, h=h):
                return g.at[owner, pa, pb] if h == 0 else g.at[owner, pb, pa]

            def share(pa, pb, view=view):
                return net.copy(view(pa, pb), view(pa, pb, owner=1), partner)

            st.append(dict(view=view, share=share, a=a, b=b))
        mid, rest = pl.ds(1, 2), pl.ds(1, 3)

        def spread(s, pa):
            return [net.copy(s["view"](pa, 0), s["view"](pa, d), ring[s["b"]][BACK[d]]) for d in (3, 1, 2)]

        for s in st:
            v = s["view"]
            s["near"] = [net.copy(v(0, 0), v(d, 0), ring[s["a"]][BACK[d]]) for d in (3, 1, 2)]
        for s in st:
            s["own"] = spread(s, 0)
            s["part"] = [s["share"](0, 0)]
        yield
        for s in st:
            s["near"][1].wait_recv()
            s["near"][2].wait_recv()
            s["mid"] = spread(s, mid)
        for s in st:
            s["near"][0].wait_recv()
            s["far"] = spread(s, 3)
            s["part"].append(s["share"](rest, 0))
        yield
        for s in st:
            for made in s["own"]:
                made.wait_recv()
            s["part"].append(s["share"](0, rest))
        yield
        for s in st:
            for made in s["mid"]:
                made.wait_recv()
            s["part"].append(s["share"](mid, rest))
        for s in st:
            for made in s["far"]:
                made.wait_recv()
            s["part"].append(s["share"](3, rest))
        yield
        for s in st:
            for made in s["part"]:
                made.wait_recv()

    def ring_sum(axis, view, landing):
        made = [net.copy(view(d), landing.at[BACK[d] - 1], ring[axis][d]) for d in (3, 1, 2)]
        yield
        for one in made:
            one.wait_recv()

    def shard_of(g, k):
        px, pz = (g // (4 * tokens_in)) % 4, (g // tokens_in) % 4
        own = g // (16 * tokens_in)
        column = source(x, px) * 8 + source(z, pz) * 2 + (core + own) % 2
        return ((g // 4) % shards_in + k * shards_in) * 32 + column

    def wanted_slots(k, want, want_t):
        g = lax.broadcasted_iota(jnp.int32, (8, gathered), 1)
        shard = jnp.broadcast_to(shard_of(g, k)[:1], (rows, gathered))
        p = lax.broadcasted_iota(jnp.int32, (rows, gathered), 0)
        want[...] = jnp.where(shard == (p >> 1) + k * (rows // 2), p & 1, -2).astype(F32)
        g = lax.broadcasted_iota(jnp.int32, (half, LANES), 0)
        shard = jnp.broadcast_to(shard_of(g, k)[:, :1], (half, rows))
        q = lax.broadcasted_iota(jnp.int32, (half, rows), 1)
        want_t[...] = jnp.where(shard == (q >> 1) + k * (rows // 2), q & 1, -2).astype(F32)

    def make_selectors(want, want_t, sel, sel_t, big):
        given = big[0][:, :, :, :, 1024:1152].reshape(gathered, LANES)
        pick = (lax.broadcasted_iota(jnp.int32, (rows, LANES), 1) == atom).astype(BF)
        sel[...] = jnp.where(nt_dot(pick, given) == want[...], 1.0, 0.0).astype(BF)
        for side in range(2):
            block = atom if side == 0 else atom + 1 - 2 * core
            pick = (lax.broadcasted_iota(jnp.int32, (LANES, rows), 0) == block).astype(BF)
            hit = nn_dot(given[:half], pick) == want_t[...]
            sel_t[:, side * rows : (side + 1) * rows] = jnp.where(hit, 1.0, 0.0).astype(BF)

    def chain(k):
        state = codes.at[pl.ds(k * rows, rows), :]
        sel, sel_t, start = r["sel"].at[k], r["sel_t"].at[k], r["start"].at[k]
        table, total = r["table"].at[k], r["total"].at[k]
        for it in range(ITERS):
            big = [r["g0a" if it == 0 else "g0b"].at[k], r["g1"].at[it, k]]
            part, opp, nbr = r["part"].at[it, k], r["y_opp"].at[it, k], r["y_nbr"].at[it, k]
            full, back, terms = r["full"].at[it, k], r["back"].at[it, k], r["terms"].at[it, k]
            if it == 0:
                pieces = [first[k * shards_in + j].astype(F32) for j in range(shards_in)]
                unit = jnp.concatenate(pieces, axis=0)
                start[...] = unit[:, :2048]
                unit = unit.astype(BF)
                big[0][0, 0, 0, :, :1024] = unit[:, :1024]
                big[0][0, 0, 0, :, 1024:] = unit[:, 2048:]
                big[1][0, 0, 0] = unit[:, 1024:2048]
            yield from gather(big)
            if it == 0:
                make_selectors(r["want"].at[k], r["want_t"].at[k], sel, sel_t, big)
            chosen = sel[...]
            for h in range(2):
                @pl.loop(0, 4)
                def _(n, h=h):
                    cols = pl.ds(pl.multiple_of(n * 256, 256), 256)
                    values = big[h][:, :, :, :, cols].reshape(gathered, 256)
                    out = pl.ds(pl.multiple_of(h * 1024 + n * 256, 256), 256)
                    table[:, out] = nn_dot(chosen, values).astype(BF)
            if it == 0 and k == 0:
                load.wait()

            def products(position):
                base = ((y + SHIFT[position]) % 4) * 512

                @pl.loop(0, 2)
                def _(n):
                    taken = weights[pl.ds(pl.multiple_of(base + n * 256, 256), 256), :]
                    cols = pl.ds(pl.multiple_of(n * 256, 256), 256)
                    part[position, :, cols] = nt_dot(table[...], taken).astype(BF)

            products(3)
            c_om = net.copy(part.at[3, :, lo], opp.at[0], plus["y"])
            c_op = net.copy(part.at[3, :, hi], opp.at[1], minus["y"])
            products(2)
            c_ph = net.copy(part.at[2, :, hi], nbr.at[0, :, hi], plus["y"])
            products(1)
            c_ml = net.copy(part.at[1, :, lo], nbr.at[1, :, lo], minus["y"])
            yield
            c_om.wait_recv()
            part[2, :, lo] = (part[2, :, lo].astype(F32) + opp[0].astype(F32)).astype(BF)
            c_pl = net.copy(part.at[2, :, lo], nbr.at[0, :, lo], plus["y"])
            c_op.wait_recv()
            part[1, :, hi] = (part[1, :, hi].astype(F32) + opp[1].astype(F32)).astype(BF)
            c_mh = net.copy(part.at[1, :, hi], nbr.at[1, :, hi], minus["y"])
            products(0)
            yield

            def update(cols):
                gradient = part[0, :, cols].astype(F32) + nbr[0, :, cols].astype(F32)
                gradient = gradient + nbr[1, :, cols].astype(F32)
                moved = STEP * (gradient - SPARSITY)
                if it > 0:
                    moved = moved + state[:, cols]
                moved = jnp.maximum(moved, 0.0)
                state[:, cols] = moved
                full[0, :, cols] = moved.astype(BF)

            c_ml.wait_recv()
            c_pl.wait_recv()
            update(lo)
            s1 = net.copy(full.at[0, :, lo], full.at[1, :, lo], plus["y"])
            c_ph.wait_recv()
            c_mh.wait_recv()
            update(hi)
            s2 = net.copy(full.at[0, :, hi], full.at[2, :, hi], minus["y"])
            s3 = net.copy(full.at[0, :, hi], full.at[1, :, hi], plus["y"])
            s4 = net.copy(full.at[0, :, lo], full.at[2, :, lo], minus["y"])

            def taken(position, cols):
                base = ((y + SHIFT[position]) % 4) * 512
                return weights[pl.ds(pl.multiple_of(base, 512), 512), cols]

            @pl.loop(0, 8)
            def _(n):
                cols = pl.ds(pl.multiple_of(n * 256, 256), 256)
                total[:, cols] = nn_dot(full[0], taken(0, cols))

            yield
            s1.wait_recv()
            f1 = net.copy(full.at[1, :, lo], full.at[3, :, lo], plus["y"])
            s2.wait_recv()
            f2 = net.copy(full.at[2, :, hi], full.at[3, :, hi], minus["y"])
            yield
            s3.wait_recv()
            s4.wait_recv()

            @pl.loop(0, 8)
            def _(n):
                cols = pl.ds(pl.multiple_of(n * 256, 256), 256)
                total[:, cols] += nn_dot(full[1], taken(1, cols)) + nn_dot(full[2], taken(2, cols))

            yield
            f1.wait_recv()
            f2.wait_recv()
            shared = []
            for quarter in range(4):
                @pl.loop(0, 2)
                def _(n, quarter=quarter):
                    cols = pl.ds(pl.multiple_of(quarter * 512 + n * 256, 256), 256)
                    done = total[:, cols] + nn_dot(full[3], taken(3, cols))
                    back[0, :, cols] = done.astype(BF)

                cols = pl.ds(quarter * 512, 512)
                shared.append(net.copy(back.at[0, :, cols], back.at[1, :, cols], partner))
            yield
            spread = sel_t[...]
            nbr_t, nbr_u, lines = r["t_nbr"].at[it, k], r["u_nbr"].at[it, k], r["lines"].at[it, k]
            sums = []
            for h in range(2):
                for made in shared[2 * h : 2 * h + 2]:
                    made.wait_recv()

                @pl.loop(0, 4)
                def _(n, h=h):
                    cols = pl.ds(pl.multiple_of(h * 1024 + n * 256, 256), 256)
                    both = nn_dot(spread[:, :rows], back[0, :, cols])
                    both = both + nn_dot(spread[:, rows:], back[1, :, cols])
                    out = pl.ds(pl.multiple_of(n * 256, 256), 256)
                    terms[h, :, :, :, out] = both.astype(BF).reshape(4, 4, tokens_in, 256)

                def term(position, h=h):
                    return terms.at[h, :, position] if h == 0 else terms.at[h, position]

                step = ring_sum("z" if h == 0 else "x", term, nbr_t.at[h])
                next(step)
                sums.append(step)
            yield
            small = []
            for h in range(2):
                for _ in sums[h]:
                    pass
                line = (terms[h, :, 0] if h == 0 else terms[h, 0]).astype(F32)
                for d in range(3):
                    line = line + nbr_t[h, d].astype(F32)
                lines[h] = line.astype(BF)

                def unit_of(position, h=h):
                    return lines.at[h, position]

                step = ring_sum("x" if h == 0 else "z", unit_of, nbr_u.at[h])
                next(step)
                small.append(step)
            yield
            for h in range(2):
                for _ in small[h]:
                    pass
                summed = lines[h, 0].astype(F32)
                for d in range(3):
                    summed = summed + nbr_u[h, d].astype(F32)
                residual = start[:, h * 1024 : (h + 1) * 1024] - summed
                if it + 1 < ITERS:
                    nxt = r["g0b"].at[k] if h == 0 else r["g1"].at[it + 1, k]
                    nxt[0, 0, 0] = residual.astype(BF)
                else:
                    for j in range(shards_in):
                        r["final"][k * shards_in + j, :, h * 1024 : (h + 1) * 1024] = residual[4 * j : 4 * j + 4]

    for k in range(CHAINS):
        wanted_slots(k, r["want"].at[k], r["want_t"].at[k])
    for made in swaps:
        made.wait_recv()
    runs = [chain(k) for k in range(CHAINS)]
    for run in runs:
        for _ in run:
            pass
    final, landed = r["final"], r["landed"]
    ends = []
    for position in (1, 2, 3):
        target = (y + SHIFT[position]) % 4
        ends.append(net.copy(final.at[target], landed.at[y], ring["y"][position]))
    landed[y] = final[y]
    for made in ends:
        made.wait_recv()
    for q in range(4):
        res_out[:, q * 2048 : (q + 1) * 2048] = landed[q]
    net.finish()


def scratch():
    t, rows, gathered = 16 // CHAINS, 256 // CHAINS, 512 // CHAINS
    c, i = CHAINS, ITERS
    v = pltpu.VMEM
    return dict(
        weights=v((2048, 2048), BF),
        first=v((4, 4, 2176), BF),
        start=v((c, t, 2048), F32),
        g0a=v((c, 2, 4, 4, t, 1152), BF),
        g0b=v((c, 2, 4, 4, t, 1024), BF),
        g1=v((i, c, 2, 4, 4, t, 1024), BF),
        sel=v((c, rows, gathered), BF),
        sel_t=v((c, gathered // 2, 2 * rows), BF),
        table=v((c, rows, 2048), BF),
        part=v((i, c, 4, rows, 512), BF),
        y_opp=v((i, c, 2, rows, 256), BF),
        y_nbr=v((i, c, 2, rows, 512), BF),
        full=v((i, c, 4, rows, 512), BF),
        total=v((c, rows, 2048), F32),
        back=v((i, c, 2, rows, 2048), BF),
        terms=v((i, c, 2, 4, 4, t, 1024), BF),
        t_nbr=v((i, c, 2, 3, 4, t, 1024), BF),
        lines=v((i, c, 2, 4, t, 1024), BF),
        u_nbr=v((i, c, 2, 3, t, 1024), BF),
        tags=v((4, LANES), BF),
        want=v((c, rows, gathered), F32),
        want_t=v((c, gathered // 2, rows), F32),
        final=v((4, 4, 2048), F32),
        landed=v((4, 4, 2048), F32),
        send=pltpu.SemaphoreType.DMA((N_SEMS,)),
        recv=pltpu.SemaphoreType.DMA((N_SEMS,)),
        wsem=pltpu.SemaphoreType.DMA,
    )


def per_device(tokens, dictionary, candidates):
    shapes = scratch()
    names = ["tok", "dict", "cand", "res", "codes"] + list(shapes)
    vmem = pl.BlockSpec(memory_space=pltpu.VMEM)
    res, codes = pl.pallas_call(
        lambda *refs: body(names, *refs),
        out_shape=(
            jax.ShapeDtypeStruct((4, 8192), F32),
            jax.ShapeDtypeStruct((256, 512), F32),
        ),
        in_specs=[vmem, pl.BlockSpec(memory_space=pl.ANY), vmem],
        out_specs=(vmem, vmem),
        scratch_shapes=list(shapes.values()),
        compiler_params=pltpu.CompilerParams(
            collective_id=0, has_side_effects=True, vmem_limit_bytes=60 * 1024 * 1024
        ),
        name="sparse_code",
    )(tokens, dictionary, candidates)
    return res, codes[None]


def solution(mesh):
    placed = (P(("grp", "atom"), None), P("atom", None, "grp"), P(("grp", "atom"), None))
    return jax.shard_map(
        per_device,
        mesh=mesh,
        in_specs=placed,
        out_specs=(P(("grp", "atom"), None), P("atom", None, "grp")),
        check_vma=False,
    )
```

time: 145 us -> 127 us (0.88)
  Pallas kernels: 138 us -> 123 us
  other arithmetic: 1.54 us -> 0 us
    pallas_call x1, Pallas kernels: 138 us -> 123 us  [per_device(): pl.pallas_call(lambda *refs: body(names, *refs), out_shape=(jax.ShapeDtyp...]
where the time goes in v2:
time: 127 us
  Pallas kernels  123 us (97%)
  local copies, waits for them, and re-layouts  3.44 us (3%)
    pallas_call x1, Pallas kernels, per_device(): pl.pallas_call(lambda *refs: body(names, *refs), out_shape=(jax.ShapeDtyp...  123 us
    unnamed x2, local copies, waits for them, and re-layouts  3.44 us

profile of v2, /device:TPU:0, one launch (start us, length us, event | category | flops | bytes accessed | tf_op | source)
XLA Modules:
  0.0 127.3 jit_solution(9212273156248093737)
XLA Ops:
  0.6 123.2 %sparse_code.1 = (f32[4,8192]{1,0:T(4,128)}, f32[256,512]{1,0:T(8,128)}) custom-call(bf16[4,8192]{1,0:T(4,128)(2,1)} %refs_0_.1, bf16[1,2048,2048]{2,1,0:T(8,128)(2,1)} %refs_1_.1, s32[4,8]{1,0:T(4,128)} %refs_2_.1), custom_call_target="tpu_custom_call" | custom-call | tf_op jit(solution)/shard_map/sparse_code/pallas_call | solution.py:426
  123.8 1.6 %copy.7 = f32[4,8192]{1,0:T(4,128)} copy(f32[4,8192]{1,0:T(4,128)} %get-tuple-element.8) | data formatting | bytes 262144
  125.4 1.9 %copy.8 = f32[1,256,512]{2,1,0:T(8,128)} copy(f32[1,256,512]{2,1,0:T(8,128)} %bitcast.1) | data formatting | bytes 1048576

commit v3 on v2

--- a/solution.py
+++ b/solution.py
@@ -152,24 +152,18 @@
                 made.wait_recv()
             s["part"].append(s["share"](0, rest))
         yield
-        for s in st:
-            for made in s["mid"]:
-                made.wait_recv()
-            s["part"].append(s["share"](mid, rest))
-        for s in st:
-            for made in s["far"]:
-                made.wait_recv()
-            s["part"].append(s["share"](3, rest))
+        for group, pa in (("mid", mid), ("far", 3)):
+            for i, d in ((1, 1), (2, 2), (0, 3)):
+                for s in st:
+                    s[group][i].wait_recv()
+                    s["part"].append(s["share"](pa, d))
         yield
         for s in st:
             for made in s["part"]:
                 made.wait_recv()
 
     def ring_sum(axis, view, landing):
-        made = [net.copy(view(d), landing.at[BACK[d] - 1], ring[axis][d]) for d in (3, 1, 2)]
-        yield
-        for one in made:
-            one.wait_recv()
+        return [net.copy(view(d), landing(BACK[d] - 1), ring[axis][d]) for d in (3, 1, 2)]
 
     def shard_of(g, k):
         px, pz = (g // (4 * tokens_in)) % 4, (g // tokens_in) % 4
@@ -218,7 +212,7 @@
                 make_selectors(r["want"].at[k], r["want_t"].at[k], sel, sel_t, big)
             chosen = sel[...]
             for h in range(2):
-                @pl.loop(0, 4)
+                @pl.loop(0, 4, unroll=True)
                 def _(n, h=h):
                     cols = pl.ds(pl.multiple_of(n * 256, 256), 256)
                     values = big[h][:, :, :, :, cols].reshape(gathered, 256)
@@ -230,7 +224,7 @@
             def products(position):
                 base = ((y + SHIFT[position]) % 4) * 512
 
-                @pl.loop(0, 2)
+                @pl.loop(0, 2, unroll=True)
                 def _(n):
                     taken = weights[pl.ds(pl.multiple_of(base + n * 256, 256), 256), :]
                     cols = pl.ds(pl.multiple_of(n * 256, 256), 256)
@@ -259,8 +253,11 @@
                 moved = STEP * (gradient - SPARSITY)
                 if it > 0:
                     moved = moved + state[:, cols]
+                if it + 1 == ITERS:
+                    state[:, cols] = moved
                 moved = jnp.maximum(moved, 0.0)
-                state[:, cols] = moved
+                if it + 1 < ITERS:
+                    state[:, cols] = moved
                 full[0, :, cols] = moved.astype(BF)
 
             c_ml.wait_recv()
@@ -278,7 +275,7 @@
                 base = ((y + SHIFT[position]) % 4) * 512
                 return weights[pl.ds(pl.multiple_of(base, 512), 512), cols]
 
-            @pl.loop(0, 8)
+            @pl.loop(0, 8, unroll=True)
             def _(n):
                 cols = pl.ds(pl.multiple_of(n * 256, 256), 256)
                 total[:, cols] = nn_dot(full[0], taken(0, cols))
@@ -292,7 +289,7 @@
             s3.wait_recv()
             s4.wait_recv()
 
-            @pl.loop(0, 8)
+            @pl.loop(0, 8, unroll=True)
             def _(n):
                 cols = pl.ds(pl.multiple_of(n * 256, 256), 256)
                 total[:, cols] += nn_dot(full[1], taken(1, cols)) + nn_dot(full[2], taken(2, cols))
@@ -302,7 +299,7 @@
             f2.wait_recv()
             shared = []
             for quarter in range(4):
-                @pl.loop(0, 2)
+                @pl.loop(0, 2, unroll=True)
                 def _(n, quarter=quarter):
                     cols = pl.ds(pl.multiple_of(quarter * 512 + n * 256, 256), 256)
                     done = total[:, cols] + nn_dot(full[3], taken(3, cols))
@@ -318,7 +315,7 @@
                 for made in shared[2 * h : 2 * h + 2]:
                     made.wait_recv()
 
-                @pl.loop(0, 4)
+                @pl.loop(0, 4, unroll=True)
                 def _(n, h=h):
                     cols = pl.ds(pl.multiple_of(h * 1024 + n * 256, 256), 256)
                     both = nn_dot(spread[:, :rows], back[0, :, cols])
@@ -326,42 +323,53 @@
                     out = pl.ds(pl.multiple_of(n * 256, 256), 256)
                     terms[h, :, :, :, out] = both.astype(BF).reshape(4, 4, tokens_in, 256)
 
-                def term(position, h=h):
-                    return terms.at[h, :, position] if h == 0 else terms.at[h, position]
-
-                step = ring_sum("z" if h == 0 else "x", term, nbr_t.at[h])
-                next(step)
-                sums.append(step)
+                rest = pl.ds(1, 3)
+                turn = []
+                for lead in (rest, 0):
+
+                    def term(position, h=h, lead=lead):
+                        return terms.at[h, lead, position] if h == 0 else terms.at[h, position, lead]
+
+                    def land(side, h=h, lead=lead):
+                        return nbr_t.at[h, side, lead]
+
+                    turn.append(ring_sum("z" if h == 0 else "x", term, land))
+                sums.append(turn)
             yield
             small = []
             for h in range(2):
-                for _ in sums[h]:
-                    pass
-                line = (terms[h, :, 0] if h == 0 else terms[h, 0]).astype(F32)
+                for made in sums[h][0]:
+                    made.wait_recv()
+                line = (terms[h, 1:4, 0] if h == 0 else terms[h, 0, 1:4]).astype(F32)
                 for d in range(3):
-                    line = line + nbr_t[h, d].astype(F32)
-                lines[h] = line.astype(BF)
+                    line = line + nbr_t[h, d, 1:4].astype(F32)
+                lines[h, 1:4] = line.astype(BF)
 
                 def unit_of(position, h=h):
                     return lines.at[h, position]
 
-                step = ring_sum("x" if h == 0 else "z", unit_of, nbr_u.at[h])
-                next(step)
-                small.append(step)
+                def land(side, h=h):
+                    return nbr_u.at[h, side]
+
+                small.append(ring_sum("x" if h == 0 else "z", unit_of, land))
             yield
             for h in range(2):
-                for _ in small[h]:
-                    pass
-                summed = lines[h, 0].astype(F32)
+                for made in sums[h][1]:
+                    made.wait_recv()
+                summed = terms[h, 0, 0].astype(F32)
+                for d in range(3):
+                    summed = summed + nbr_t[h, d, 0].astype(F32)
+                for made in small[h]:
+                    made.wait_recv()
                 for d in range(3):
                     summed = summed + nbr_u[h, d].astype(F32)
-                residual = start[:, h * 1024 : (h + 1) * 1024] - summed
                 if it + 1 < ITERS:
+                    residual = start[:, h * 1024 : (h + 1) * 1024] - summed
                     nxt = r["g0b"].at[k] if h == 0 else r["g1"].at[it + 1, k]
                     nxt[0, 0, 0] = residual.astype(BF)
                 else:
                     for j in range(shards_in):
-                        r["final"][k * shards_in + j, :, h * 1024 : (h + 1) * 1024] = residual[4 * j : 4 * j + 4]
+                        r["final"][k * shards_in + j, :, h * 1024 : (h + 1) * 1024] = summed[4 * j : 4 * j + 4]
 
     for k in range(CHAINS):
         wanted_slots(k, r["want"].at[k], r["want_t"].at[k])
@@ -423,7 +431,7 @@
     shapes = scratch()
     names = ["tok", "dict", "cand", "res", "codes"] + list(shapes)
     vmem = pl.BlockSpec(memory_space=pltpu.VMEM)
-    res, codes = pl.pallas_call(
+    rebuilt, codes = pl.pallas_call(
         lambda *refs: body(names, *refs),
         out_shape=(
             jax.ShapeDtypeStruct((4, 8192), F32),
@@ -437,7 +445,7 @@
         ),
         name="sparse_code",
     )(tokens, dictionary, candidates)
-    return res, codes[None]
+    return tokens.astype(F32) - rebuilt, jnp.maximum(codes, 0.0)[None]
 
 
 def solution(mesh):

time: 127 us -> 120 us (0.945)
  Pallas kernels: 123 us -> 115 us
  other arithmetic: 0 us -> 3.47 us
  local copies, waits for them, and re-layouts: 3.44 us -> 0.01 us
    pallas_call x1, Pallas kernels: 123 us -> 115 us  [per_device(): pl.pallas_call(lambda *refs: body(names, *refs), out_shape=(jax.ShapeDtyp...]
    unnamed x2, local copies, waits for them, and re-layouts: 3.44 us -> 0.01 us
    broadcast_in_dim x0 -> x1, other arithmetic: none -> 1.87 us  [per_device(): return (tokens.astype(F32) - rebuilt, jnp.maximum(codes, 0.0)[None])]
    sub x0 -> x1, other arithmetic: none -> 1.6 us  [per_device(): return (tokens.astype(F32) - rebuilt, jnp.maximum(codes, 0.0)[None])]
where the time goes in v3:
time: 120 us
  Pallas kernels  115 us (96%)
  other arithmetic  3.47 us (3%)
    pallas_call x1, Pallas kernels, per_device(): pl.pallas_call(lambda *refs: body(names, *refs), out_shape=(jax.ShapeDtyp...  115 us

profile of v3, /device:TPU:0, one launch (start us, length us, event | category | flops | bytes accessed | tf_op | source)
XLA Modules:
  0.0 119.5 jit_solution(8058425879123756701)
XLA Ops:
  0.6 0.0 copy-start
  0.6 115.4 %sparse_code.1 = (f32[4,8192]{1,0:T(4,128)}, f32[256,512]{1,0:T(8,128)}) custom-call(bf16[4,8192]{1,0:T(4,128)(2,1)} %refs_0_.1, bf16[1,2048,2048]{2,1,0:T(8,128)(2,1)} %refs_1_.1, s32[4,8]{1,0:T(4,128)} %refs_2_.1), custom_call_target="tpu_custom_call" | custom-call | tf_op jit(solution)/shard_map/sparse_code/pallas_call | solution.py:434
  116.0 0.0 copy-done
  116.0 1.6 %convert_subtract_fusion = f32[4,8192]{1,0:T(4,128)} fusion(f32[4,8192]{1,0:T(4,128)} %get-tuple-element.4, bf16[4,8192]{1,0:T(4,128)(2,1)S(1)} %copy-done), kind=kLoop, calls=%fused_computation.1 | loop fusion | flops 65536 | bytes 327680 | tf_op jit(solution)/shard_map/sub | solution.py:448
  117.6 1.9 %maximum_bitcast_fusion = f32[1,256,512]{2,1,0:T(8,128)} fusion(f32[256,512]{1,0:T(8,128)} %get-tuple-element.5), kind=kLoop, calls=%fused_computation | loop fusion | flops 131072 | bytes 1048576 | tf_op jit(solution)/shard_map/broadcast_in_dim | solution.py:448
Async XLA Ops:
  0.6 115.4 %copy-start = (bf16[4,8192]{1,0:T(4,128)(2,1)S(1)}, bf16[4,8192]{1,0:T(4,128)(2,1)}, u32[]{:S(2)}) copy-start(bf16[4,8192]{1,0:T(4,128)(2,1)} %refs_0_.1) | copy-start | bytes 196612
